TPU v7x, 512 devices: a whole 4x4x16 slice. The times are simulated.
512 devices in a mesh: pairs: 64 (over x, z), grp: 8 (over y, core).
Axes of the slice: x: 4, y: 4, z: 16, core: 2. Of those that a mesh axis runs over, the one named last changes fastest.
Arguments:
- spectra: bfloat16 [8192, 1, 2048], P(('pairs', 'grp')), as said below
- row_station: int32 [8192], P(('pairs', 'grp')), may hold values from 0 to 4095, as said below
- row_window: int32 [8192], P(('pairs', 'grp')), may hold values from 0 to 1, as said below
- station_owner: int32 [4096], replicated, may hold values from 0 to 511, as said below
- tile_stations: int32 [64, 384], replicated, may hold values from 0 to 4095, as said below
- pair_index: int32 [64, 8, 2, 48], P('pairs', 'grp'), may hold values from 0 to 383
Outputs:
- correlation: float32 [64, 8, 48, 2001], P('pairs', 'grp')
Inputs may be any that keep to these rules, and one draw needn't show every extreme that they name: `row_station`: every station's 2 windows lie on the device that station_owner names, one row each; every device holds 8 stations. `row_window`: A device's rows of one station carry each window number once. `station_owner`: devices are numbered by pairs index times the size of grp plus grp index. `tile_stations`: A group's list holds distinct stations on distinct devices; exactly 48 of them lie on devices of each grp index. `spectra`: real parts of the 1024 bins, then their imaginary parts.
All inputs are finite; a program needn't handle non-finite values.
Results may differ from a plain program's by a relative error of at most 0.0056.
Values may be sent and summed in bfloat16 or wider, within the bound.
A program may use at most 64 MiB of HBM per device.

v0:
```python
import math
import jax
import jax.numpy as jnp
from jax import lax
from jax.sharding import PartitionSpec as P

W = 2
NSEG = 1
NFFT = 2048
BAND = 128
MAXLAG = 1000
LAGS = 2001
freq_block_max = 512
power_eps = 1e-06


def whiten_rows(spectra, band_width):
    half_bins = spectra.shape[-1] // 2
    leading = spectra.shape[:-1]
    values = spectra.astype(jnp.float32).reshape(leading + (2, half_bins // band_width, band_width))
    band_power = jnp.mean(jnp.sum(values * values, axis=-3), axis=-1)
    scaling = lax.rsqrt(band_power + power_eps)
    whitened = values * scaling[..., None, :, None]
    return whitened.reshape(spectra.shape).astype(jnp.bfloat16)


def lag_table(offset, bin_count):
    freq_index = (offset + jnp.arange(bin_count, dtype=jnp.int32))[:, None]
    lag_shift = (jnp.arange(LAGS, dtype=jnp.int32) + (NFFT - MAXLAG))[None, :]
    angles = (freq_index * lag_shift % NFFT).astype(jnp.float32) * (2.0 * math.pi / NFFT)
    return jnp.concatenate([jnp.cos(angles), -jnp.sin(angles)], axis=0).astype(jnp.bfloat16)


def cross_block(source_rows, first_rows, second_rows, offset, bin_count):
    half_bins = source_rows.shape[-1] // 2
    real_part = source_rows[:, :, offset : offset + bin_count]
    imag_part = source_rows[:, :, half_bins + offset : half_bins + offset + bin_count]
    real_a = real_part[first_rows].astype(jnp.float32)
    imag_a = imag_part[first_rows].astype(jnp.float32)
    real_b = real_part[second_rows].astype(jnp.float32)
    imag_b = imag_part[second_rows].astype(jnp.float32)
    cross_real = jnp.sum(real_a * real_b + imag_a * imag_b, axis=(1, 2))
    cross_imag = jnp.sum(imag_a * real_b - real_a * imag_b, axis=(1, 2))
    return jnp.concatenate([cross_real, cross_imag], axis=1).astype(jnp.bfloat16)


def correlate(source_rows, first_rows, second_rows):
    half_bins = NFFT // 2
    block_size = min(freq_block_max, half_bins)
    running = jnp.zeros((first_rows.shape[0], LAGS), jnp.float32)
    for offset in range(0, half_bins, block_size):
        cross_terms = cross_block(source_rows, first_rows, second_rows, offset, block_size)
        running = running + jnp.dot(
            cross_terms, lag_table(offset, block_size), preferred_element_type=jnp.float32
        )
    return running * (1.0 / math.sqrt(half_bins * W * NSEG))


def on_device(spectra, row_station, row_window, station_owner, tile_stations, pair_index):
    group_count = lax.axis_size("grp")
    pair_groups = lax.axis_size("pairs")
    my_pair = lax.axis_index("pairs")
    local_count = spectra.shape[0]
    row_tail = spectra.shape[1:]
    window_ids = jnp.arange(W, dtype=jnp.int32)
    local_ids = jnp.arange(local_count, dtype=jnp.int32)
    zero_value = jnp.zeros((), jnp.bfloat16)
    whitened = whiten_rows(spectra, BAND)
    my_tile = lax.dynamic_index_in_dim(tile_stations, my_pair, 0, keepdims=False)
    tile_owner = station_owner[my_tile]
    pooled, pooled_station, pooled_window = (
        lax.all_gather(whitened, "grp", axis=0, tiled=True),
        lax.all_gather(row_station, "grp", axis=0, tiled=True),
        lax.all_gather(row_window, "grp", axis=0, tiled=True),
    )
    wanted = jnp.any(pooled_station[None, :, None] == tile_stations[:, None, :], axis=2)
    wanted = wanted.reshape(pair_groups, group_count, 1, local_count)
    window_hit = (
        pooled_window.reshape(group_count, local_count)[:, None, :] == window_ids[None, :, None]
    )[None]
    selected = wanted & window_hit
    position = jnp.sum(jnp.where(selected, local_ids, 0), axis=3)
    position = position + (jnp.arange(group_count, dtype=jnp.int32) * local_count)[None, :, None]
    present = jnp.any(selected, axis=3)
    outgoing = jnp.where(present.reshape(-1, 1, 1), pooled[position.reshape(-1)], zero_value)
    outgoing = outgoing.reshape((pair_groups, group_count * W) + row_tail)
    arrived = lax.all_to_all(outgoing, "pairs", split_axis=0, concat_axis=0, tiled=True)
    source_rows = arrived.reshape((-1,) + row_tail)
    row_base = tile_owner * W
    pair_lists = pair_index.reshape(2, -1)
    first_rows = row_base[pair_lists[0]][:, None] + window_ids[None, :]
    second_rows = row_base[pair_lists[1]][:, None] + window_ids[None, :]
    running = correlate(source_rows, first_rows, second_rows)
    return running.reshape((pair_index.shape[0], pair_index.shape[1], pair_index.shape[3], LAGS))


def solution(mesh):
    placed = (
        P(("pairs", "grp"), None, None),
        P(("pairs", "grp")),
        P(("pairs", "grp")),
        P(),
        P(),
        P("pairs", "grp", None, None),
    )
    return jax.shard_map(
        on_device,
        mesh=mesh,
        in_specs=placed,
        out_specs=P("pairs", "grp", None, None),
        check_vma=False,
    )
```

profile of v0, /device:TPU:38, one launch (start us, length us, event | category | flops | bytes accessed | tf_op | source)
XLA Modules:
  0.0 268.8 jit_solution(16281639147075482824)
XLA Ops:
  0.0 0.0 copy-start
  0.0 1.3 dynamic-slice
  1.9 0.9 dynamic-update-slice.1
  2.8 0.8 dynamic-update-slice
  3.6 9.5 %all-reduce.2 = (s32[128]{0:T(128)S(1)}, s32[128]{0:T(128)S(1)}) all-reduce(s32[128]{0:T(128)S(1)} %dynamic-update-slice.1, s32[128]{0:T(128)S(1)} %dynamic-update-slice), channel_id=1, replica_groups=mesh['pairs'=64,'grp'=8] {'grp'}, use_global_device_ids=true, to_apply=%add.1 | all-reduce | flops 256 | bytes 2048
  13.1 0.1 eq.38
  13.2 2.1 compare_reduce_fusion
  15.3 0.1 copy.16
  15.5 0.1 and_reduce_fusion
  15.6 0.1 fusion.32
  15.7 0.1 copy.17
  15.9 0.9 fusion.30
  16.7 0.1 reduce_sum.58
  16.9 0.1 mul.188
  17.0 0.9 fusion.31
  17.8 0.1 copy_add_fusion
  17.9 0.2 copy.19
  18.1 0.2 add.216
  18.3 13.1 %all_gather.11 = bf16[128,1,2048]{2,0,1:T(8,128)(2,1)S(1)} all-gather(bf16[16,1,2048]{2,0,1:T(8,128)(2,1)S(1)} %fusion.31), channel_id=1, replica_groups=mesh['pairs'=64,'grp'=8] {'grp'}, dimensions={0}, use_global_device_ids=true | all-gather | bytes 589824 | tf_op jit(solution)/shard_map/all_gather | solution.py:72
  31.4 6.0 %gather_fusion = bf16[1024,2048]{1,0:T(8,128)(2,1)} fusion(bf16[128,2048]{1,0:T(8,128)(2,1)S(1)} %bitcast.42, s32[1024]{0:T(1024)S(1)} %broadcast_clamp_fusion), kind=kCustom, calls=%fused_computation | custom fusion | bytes 8392704 | tf_op jit(solution)/shard_map/gather | solution.py:85
  37.4 4.5 %broadcast_select_fusion = bf16[64,16,1,2048]{3,1,2,0:T(8,128)(2,1)} fusion(bf16[64,16,1,2048]{3,1,2,0:T(8,128)(2,1)} %bitcast.43, pred[64,16]{1,0:T(8,128)(4,1)S(1)} %copy.17), kind=kLoop, calls=%fused_computation.42 | loop fusion | flops 2097152 | bytes 8389632 | tf_op jit(solution)/shard_map/jit(_where)/select_n | solution.py:85
  41.9 0.0 copy-start.3
  42.0 18.7 %all-to-all-start = ((bf16[64,16,1,2048]{3,1,2,0:T(8,128)(2,1)}), bf16[64,16,1,2048]{3,1,2,0:T(8,128)(2,1)}, u32[]{:S(2)}, u32[]{:S(2)}) async-start(bf16[64,16,1,2048]{3,1,2,0:T(8,128)(2,1)} %broadcast_select_fusion), calls=%async_computation | async-start | bytes 8388608 | tf_op jit(solution)/shard_map/all_to_all | solution.py:87
  60.6 0.7 fusion.39
  61.4 0.0 copy-done
  61.4 2.5 gather_fusion.1
  63.9 0.0 copy-done.3
  64.0 0.8 gather_fusion.4
  64.8 0.8 gather_fusion.2
  65.6 0.1 compare_select_fusion.1
  65.7 0.1 reshape.431
  65.8 0.1 compare_select_fusion
  65.9 0.1 reshape.449
  66.0 36.1 %cosine_convert_fusion = (bf16[512,2001]{1,0:T(8,128)(2,1)}, bf16[512,2001]{1,0:T(8,128)(2,1)}, bf16[512,2001]{1,0:T(8,128)(2,1)}, bf16[512,2001]{1,0:T(8,128)(2,1)}) fusion(s32[2001]{0:T(1024)S(1)} %iota_add_fusion, s32[512]{0:T(512)S(1)} %iota_add_fusion.1), kind=kLoop, calls=%fused_computation.36 | loop fusion | flops 34833408 | bytes 8206148 | tf_op jit(solution)/shard_map/convert
  102.1 146.1 %all-to-all-done = bf16[64,16,1,2048]{3,1,2,0:T(8,128)(2,1)} async-done(((bf16[64,16,1,2048]{3,1,2,0:T(8,128)(2,1)}), bf16[64,16,1,2048]{3,1,2,0:T(8,128)(2,1)}, u32[]{:S(2)}, u32[]{:S(2)}) %all-to-all-start) | async-done | bytes 4194336 | tf_op jit(solution)/shard_map/all_to_all | solution.py:87
  248.2 3.6 %slice_bitcast_fusion = (bf16[1024,512]{1,0:T(8,128)(2,1)}, bf16[1024,512]{1,0:T(8,128)(2,1)S(1)}, bf16[1024,512]{1,0:T(8,128)(2,1)S(1)}, bf16[1024,512]{1,0:T(8,128)(2,1)S(1)}) fusion(bf16[1024,1,2048]{2,0,1:T(8,128)(2,1)} %bitcast.6), kind=kLoop, calls=%fused_computation.46 | loop fusion | bytes 8388608 | tf_op jit(solution)/shard_map/slice | solution.py:37
  251.8 2.2 gather_fusion.11
  254.0 2.2 gather_fusion.10
  256.1 0.8 gather_fusion.9
  256.9 1.4 gather_fusion.8
  258.3 0.8 gather_fusion.7
  259.1 0.8 gather_fusion.6
  259.9 0.8 gather_fusion.3
  260.6 0.8 gather_fusion.5
  261.4 1.0 fusion.28
  262.4 0.1 reshape.562
  262.5 0.2 reduce_sum.62
  262.7 0.1 fusion.26
  262.8 0.1 reshape.560
  262.9 0.0 copy-start.1
  262.9 0.2 reduce_sum.60
  263.2 0.1 reshape.561
  263.3 0.2 reduce_sum.61
  263.6 0.1 reshape.563
  263.7 0.2 reduce_sum.63
  263.9 0.0 copy-start.2
  263.9 3.2 %fusion.6 = f32[48,2001]{1,0:T(8,128)S(1)} fusion(bf16[512,2001]{1,0:T(8,128)(2,1)} %get-tuple-element.17, bf16[512,2001]{1,0:T(8,128)(2,1)} %get-tuple-element.18, bf16[48,512]{1,0:T(8,128)(2,1)S(1)} %reduce_sum.61, bf16[48,512]{1,0:T(8,128)(2,1)S(1)} %reduce_sum.60), kind=kOutput, calls=%fused_computation.27 | convolution fusion | flops 205099008 | bytes 4580544 | tf_op jit(solution)/shard_map/dot_general | solution.py:53
  267.1 0.0 copy-done.1
  267.2 0.0 copy-done.2
  267.2 1.6 fusion.23
  (18 shorter events, 0.2 us)
Async XLA Ops:
  0.0 61.4 %copy-start = (s32[4096]{0:T(1024)S(1)}, s32[4096]{0:T(1024)}, u32[]{:S(2)}) copy-start(s32[4096]{0:T(1024)} %param.9) | copy-start | bytes 49156
  41.9 22.0 %copy-start.3 = (s32[1,1,2,48]{3,2,1,0:T(2,128)S(1)}, s32[1,1,2,48]{3,2,1,0:T(2,128)}, u32[]{:S(2)}) copy-start(s32[1,1,2,48]{3,2,1,0:T(2,128)} %param.11) | copy-start | bytes 1156
  42.0 206.2 %all-to-all-start = ((bf16[64,16,1,2048]{3,1,2,0:T(8,128)(2,1)}), bf16[64,16,1,2048]{3,1,2,0:T(8,128)(2,1)}, u32[]{:S(2)}, u32[]{:S(2)}) async-start(bf16[64,16,1,2048]{3,1,2,0:T(8,128)(2,1)} %broadcast_select_fusion), calls=%async_computation | async-start | bytes 8388608 | tf_op jit(solution)/shard_map/all_to_all | solution.py:87
  262.9 4.2 %copy-start.1 = (bf16[512,2001]{1,0:T(8,128)(2,1)S(1)}, bf16[512,2001]{1,0:T(8,128)(2,1)}, u32[]{:S(2)}) copy-start(bf16[512,2001]{1,0:T(8,128)(2,1)} %get-tuple-element.15) | copy-start | bytes 6147076
  263.9 3.2 %copy-start.2 = (bf16[512,2001]{1,0:T(8,128)(2,1)S(1)}, bf16[512,2001]{1,0:T(8,128)(2,1)}, u32[]{:S(2)}) copy-start(bf16[512,2001]{1,0:T(8,128)(2,1)} %get-tuple-element.16) | copy-start | bytes 6147076
where the time goes:
time: 269 us
  waiting for transfers between devices  146 us (54%)
  other arithmetic  47.8 us (18%)
  local copies, waits for them, and re-layouts  27.8 us (10%)
  blocking collectives  22.6 us (8%)
  starting transfers between devices  18.7 us (7%)
  matrix products  4.81 us (2%)
    all_to_all x1, waiting for transfers between devices, on_device(): lax.all_to_all(outgoing, 'pairs', split_axis=0, concat_axis=0, tiled=True)  146 us
    another operation x1, other arithmetic  36.1 us
    all_to_all x1, starting transfers between devices, on_device(): lax.all_to_all(outgoing, 'pairs', split_axis=0, concat_axis=0, tiled=True)  18.7 us
    all_gather x1, blocking collectives, on_device(): lax.all_gather(whitened, 'grp', axis=0, tiled=True)  13.1 us
    unnamed x1, blocking collectives  9.48 us
    gather x1, local copies, waits for them, and re-layouts, on_device(): pooled[position.reshape(-1)]  6.01 us
  transfers between devices with their start and end apart: 1, of which 1 were waited for; matrix products, arithmetic and copies ran while one was open for 15% of the time, Pallas kernels for 0%

commit v1 on v0

--- a/solution.py
+++ b/solution.py
@@ -12,6 +12,13 @@
 LAGS = 2001
 freq_block_max = 512
 power_eps = 1e-06
+
+
+def gather_over(x, name, d):
+    peers = lax.axis_size(name)
+    blocks = jnp.stack([x for _ in range(peers)])
+    blocks = lax.all_to_all(blocks, name, split_axis=0, concat_axis=0)
+    return jnp.concatenate(blocks, axis=d)
 
 
 def whiten_rows(spectra, band_width):
@@ -69,7 +76,7 @@
     my_tile = lax.dynamic_index_in_dim(tile_stations, my_pair, 0, keepdims=False)
     tile_owner = station_owner[my_tile]
     pooled, pooled_station, pooled_window = (
-        lax.all_gather(whitened, "grp", axis=0, tiled=True),
+        gather_over(whitened, "grp", 0),
         lax.all_gather(row_station, "grp", axis=0, tiled=True),
         lax.all_gather(row_window, "grp", axis=0, tiled=True),
     )

time: 269 us -> 261 us (0.970)
  blocking collectives: 22.6 us -> 9.68 us
  starting transfers between devices: 18.7 us -> 23.1 us
    all_gather x1 -> x0, blocking collectives: 13.1 us -> none  [on_device(): lax.all_gather(whitened, 'grp', axis=0, tiled=True)]
    all_to_all x0 -> x1, starting transfers between devices: none -> 4.47 us  [gather_over(): blocks = lax.all_to_all(blocks, name, split_axis=0, concat_axis=0)]
  transfers between devices with their start and end apart: 1 -> 2, of which waited for: 1 -> 1; matrix products, arithmetic and copies ran while one was open for 15% -> 18% of each run, Pallas kernels for 0% -> 0%
where the time goes in v1:
time: 261 us; the launch traced here: 260 us
  waiting for transfers between devices  145 us (56%)
  other arithmetic  47.8 us (18%)
  local copies, waits for them, and re-layouts  28.7 us (11%)
  starting transfers between devices  23.1 us (9%)
  blocking collectives  9.68 us (4%)
  matrix products  4.81 us (2%)
    all_to_all x1, waiting for transfers between devices, on_device(): lax.all_to_all(outgoing, 'pairs', split_axis=0, concat_axis=0, tiled=True)  145 us
    another operation x1, other arithmetic  36.1 us
    all_to_all x1, starting transfers between devices, on_device(): lax.all_to_all(outgoing, 'pairs', split_axis=0, concat_axis=0, tiled=True)  18.7 us
    unnamed x1, blocking collectives  9.68 us
    gather x1, local copies, waits for them, and re-layouts, on_device(): pooled[position.reshape(-1)]  6.02 us
  transfers between devices with their start and end apart: 2, of which 1 were waited for; matrix products, arithmetic and copies ran while one was open for 18% of the time, Pallas kernels for 0%

profile of v1, /device:TPU:38, one launch (start us, length us, event | category | flops | bytes accessed | tf_op | source)
XLA Modules:
  0.0 259.9 jit_solution(1726767515860877633)
XLA Ops:
  0.0 0.0 copy-start
  0.0 0.9 fusion.30
  0.9 0.1 reduce_sum.58
  1.0 0.1 mul.188
  1.1 0.9 fusion.39
  2.0 0.8 stack.2
  2.8 4.5 %all-to-all-start = ((bf16[8,16,1,2048]{3,1,2,0:T(8,128)(2,1)}), bf16[8,16,1,2048]{3,1,2,0:T(8,128)(2,1)S(1)}, u32[]{:S(2)}, u32[]{:S(2)}) async-start(bf16[8,16,1,2048]{3,1,2,0:T(8,128)(2,1)} %stack.2), calls=%async_computation | async-start | bytes 1048576 | tf_op jit(solution)/shard_map/all_to_all | solution.py:20
  7.3 1.3 dynamic-slice
  9.3 0.9 dynamic-update-slice.1
  10.1 0.8 dynamic-update-slice
  11.0 9.7 %all-reduce.2 = (s32[128]{0:T(128)S(1)}, s32[128]{0:T(128)S(1)}) all-reduce(s32[128]{0:T(128)S(1)} %dynamic-update-slice.1, s32[128]{0:T(128)S(1)} %dynamic-update-slice), channel_id=1, replica_groups=mesh['pairs'=64,'grp'=8] {'grp'}, use_global_device_ids=true, to_apply=%add.1 | all-reduce | flops 256 | bytes 2048
  20.6 0.1 eq.38
  20.7 2.1 compare_reduce_fusion
  22.9 0.1 copy.16
  23.0 0.1 fusion.32
  23.1 0.1 copy_add_fusion
  23.2 0.1 and_reduce_fusion
  23.3 0.1 copy.17
  23.4 0.2 copy.19
  23.6 0.2 add.216
  23.8 0.0 all-to-all-done
  23.9 6.0 %gather_fusion = bf16[1024,2048]{1,0:T(8,128)(2,1)} fusion(bf16[128,2048]{1,0:T(8,128)(2,1)S(1)} %bitcast.44, s32[1024]{0:T(1024)S(1)} %broadcast_clamp_fusion), kind=kCustom, calls=%fused_computation | custom fusion | bytes 8392704 | tf_op jit(solution)/shard_map/gather | solution.py:92
  29.9 4.5 %broadcast_select_fusion = bf16[64,16,1,2048]{3,1,2,0:T(8,128)(2,1)} fusion(bf16[64,16,1,2048]{3,1,2,0:T(8,128)(2,1)} %bitcast.45, pred[64,16]{1,0:T(8,128)(4,1)S(1)} %copy.17), kind=kLoop, calls=%fused_computation.42 | loop fusion | flops 2097152 | bytes 8389632 | tf_op jit(solution)/shard_map/jit(_where)/select_n | solution.py:92
  34.4 0.0 copy-start.3
  34.4 18.7 %all-to-all-start.1 = ((bf16[64,16,1,2048]{3,1,2,0:T(8,128)(2,1)}), bf16[64,16,1,2048]{3,1,2,0:T(8,128)(2,1)}, u32[]{:S(2)}, u32[]{:S(2)}) async-start(bf16[64,16,1,2048]{3,1,2,0:T(8,128)(2,1)} %broadcast_select_fusion), calls=%async_computation.1 | async-start | bytes 8388608 | tf_op jit(solution)/shard_map/all_to_all | solution.py:94
  53.1 0.7 fusion.40
  53.8 0.0 copy-done
  53.8 2.5 gather_fusion.1
  56.4 0.0 copy-done.3
  56.4 0.8 gather_fusion.4
  57.2 0.8 gather_fusion.2
  58.0 0.1 compare_select_fusion.1
  58.1 0.1 reshape.438
  58.2 0.1 compare_select_fusion
  58.3 0.1 reshape.456
  58.5 36.1 %cosine_convert_fusion = (bf16[512,2001]{1,0:T(8,128)(2,1)}, bf16[512,2001]{1,0:T(8,128)(2,1)}, bf16[512,2001]{1,0:T(8,128)(2,1)}, bf16[512,2001]{1,0:T(8,128)(2,1)}) fusion(s32[2001]{0:T(1024)S(1)} %iota_add_fusion, s32[512]{0:T(512)S(1)} %iota_add_fusion.1), kind=kLoop, calls=%fused_computation.36 | loop fusion | flops 34833408 | bytes 8206148 | tf_op jit(solution)/shard_map/convert
  94.6 144.8 %all-to-all-done.1 = bf16[64,16,1,2048]{3,1,2,0:T(8,128)(2,1)} async-done(((bf16[64,16,1,2048]{3,1,2,0:T(8,128)(2,1)}), bf16[64,16,1,2048]{3,1,2,0:T(8,128)(2,1)}, u32[]{:S(2)}, u32[]{:S(2)}) %all-to-all-start.1) | async-done | bytes 4194336 | tf_op jit(solution)/shard_map/all_to_all | solution.py:94
  239.3 3.6 %slice_bitcast_fusion = (bf16[1024,512]{1,0:T(8,128)(2,1)}, bf16[1024,512]{1,0:T(8,128)(2,1)S(1)}, bf16[1024,512]{1,0:T(8,128)(2,1)S(1)}, bf16[1024,512]{1,0:T(8,128)(2,1)S(1)}) fusion(bf16[1024,1,2048]{2,0,1:T(8,128)(2,1)} %bitcast.7), kind=kLoop, calls=%fused_computation.46 | loop fusion | bytes 8388608 | tf_op jit(solution)/shard_map/slice | solution.py:44
  242.9 2.2 gather_fusion.11
  245.1 2.2 gather_fusion.10
  247.3 0.8 gather_fusion.9
  248.0 1.4 gather_fusion.8
  249.5 0.8 gather_fusion.7
  250.2 0.8 gather_fusion.6
  251.0 0.8 gather_fusion.3
  251.8 0.8 gather_fusion.5
  252.6 1.0 fusion.28
  253.5 0.1 reshape.570
  253.6 0.2 reduce_sum.62
  253.9 0.1 fusion.26
  254.0 0.1 reshape.568
  254.1 0.0 copy-start.1
  254.1 0.2 reduce_sum.60
  254.3 0.1 reshape.569
  254.5 0.2 reduce_sum.61
  254.7 0.1 reshape.571
  254.8 0.2 reduce_sum.63
  255.1 0.0 copy-start.2
  255.1 3.2 %fusion.6 = f32[48,2001]{1,0:T(8,128)S(1)} fusion(bf16[512,2001]{1,0:T(8,128)(2,1)} %get-tuple-element.17, bf16[512,2001]{1,0:T(8,128)(2,1)} %get-tuple-element.18, bf16[48,512]{1,0:T(8,128)(2,1)S(1)} %reduce_sum.61, bf16[48,512]{1,0:T(8,128)(2,1)S(1)} %reduce_sum.60), kind=kOutput, calls=%fused_computation.27 | convolution fusion | flops 205099008 | bytes 4580544 | tf_op jit(solution)/shard_map/dot_general | solution.py:60
  258.3 0.0 copy-done.1
  258.3 0.0 copy-done.2
  258.3 1.6 fusion.23
  (18 shorter events, 0.2 us)
Async XLA Ops:
  0.0 53.8 %copy-start = (s32[4096]{0:T(1024)S(1)}, s32[4096]{0:T(1024)}, u32[]{:S(2)}) copy-start(s32[4096]{0:T(1024)} %param.9) | copy-start | bytes 49156
  2.8 21.0 %all-to-all-start = ((bf16[8,16,1,2048]{3,1,2,0:T(8,128)(2,1)}), bf16[8,16,1,2048]{3,1,2,0:T(8,128)(2,1)S(1)}, u32[]{:S(2)}, u32[]{:S(2)}) async-start(bf16[8,16,1,2048]{3,1,2,0:T(8,128)(2,1)} %stack.2), calls=%async_computation | async-start | bytes 1048576 | tf_op jit(solution)/shard_map/all_to_all | solution.py:20
  34.4 22.0 %copy-start.3 = (s32[1,1,2,48]{3,2,1,0:T(2,128)S(1)}, s32[1,1,2,48]{3,2,1,0:T(2,128)}, u32[]{:S(2)}) copy-start(s32[1,1,2,48]{3,2,1,0:T(2,128)} %param.11) | copy-start | bytes 1156
  34.4 204.9 %all-to-all-start.1 = ((bf16[64,16,1,2048]{3,1,2,0:T(8,128)(2,1)}), bf16[64,16,1,2048]{3,1,2,0:T(8,128)(2,1)}, u32[]{:S(2)}, u32[]{:S(2)}) async-start(bf16[64,16,1,2048]{3,1,2,0:T(8,128)(2,1)} %broadcast_select_fusion), calls=%async_computation.1 | async-start | bytes 8388608 | tf_op jit(solution)/shard_map/all_to_all | solution.py:94
  254.1 4.2 %copy-start.1 = (bf16[512,2001]{1,0:T(8,128)(2,1)S(1)}, bf16[512,2001]{1,0:T(8,128)(2,1)}, u32[]{:S(2)}) copy-start(bf16[512,2001]{1,0:T(8,128)(2,1)} %get-tuple-element.15) | copy-start | bytes 6147076
  255.1 3.2 %copy-start.2 = (bf16[512,2001]{1,0:T(8,128)(2,1)S(1)}, bf16[512,2001]{1,0:T(8,128)(2,1)}, u32[]{:S(2)}) copy-start(bf16[512,2001]{1,0:T(8,128)(2,1)} %get-tuple-element.16) | copy-start | bytes 6147076
